TPU v7x, 128 devices: a whole 4x4x4 slice. The times are simulated.
128 devices in a mesh: corpus: 32 (over y, z, core), tensor: 4 (over x).
Axes of the slice: x: 4, y: 4, z: 4, core: 2. Of those that a mesh axis runs over, the one named last changes fastest.
Arguments:
- hidden: bfloat16 [12288, 4096], P('corpus', 'tensor'), may hold values from -6 to 6
- lengths: int32 [32, 32], P('corpus'), may hold values from 1 to 48, 384 in all within a row
- steer_ids: int32 [1024], P('corpus'), may hold values from 0 to 15
- in_gain: float32 [4096], replicated, may hold values from 0.6 to 14
- w_query: bfloat16 [4096, 2048], P(None, 'tensor'), may hold values from -0.09375 to 0.09375
- w_key: bfloat16 [4096, 1024], P(None, 'tensor'), may hold values from -0.09375 to 0.09375
- w_value: bfloat16 [4096, 1024], P(None, 'tensor'), may hold values from -0.09375 to 0.09375
- w_out: bfloat16 [2048, 4096], P('tensor'), may hold values from -0.125 to 0.125
- steer_table: bfloat16 [16, 4096], replicated, may hold values from -12 to 12
- strength: float32 [16], replicated, may hold values from 0.1 to 0.5
- out_gain: float32 [4096], replicated, may hold values from 0.1 to 1.9
- index_rows: bfloat16 [131072, 4096], P(('corpus', 'tensor')), may hold values from -6 to 6
Outputs:
- scores: bfloat16 [1024, 131072], P(None, ('corpus', 'tensor'))
Inputs may be any that keep to these rules, and one draw needn't show every extreme that they name: Each row of lengths holds the token counts of the 32 queries packed in order into the 384 tokens of one group.
All inputs are finite; a program needn't handle non-finite values.
Results may differ from a plain program's by a relative error of at most 0.005.
The roundings to bfloat16 on the way count: a program that leaves them out, or rounds other values in their place, can miss the bound.
Values may be sent and summed in bfloat16 or wider, within the bound.
No kernel may reach another device: no remote copies, remote signals or barrier semaphores. Data moves between devices by JAX's collectives and lax.ppermute only.
A program may use at most 128 MiB of HBM per device.

v0:
```python
import jax
import jax.numpy as jnp
from jax import lax
from jax.sharding import PartitionSpec as P

D = 4096
HEAD = 128
rope_base = 1000000.0


def rotate(vectors, positions):
    half_width = vectors.shape[-1] // 2
    frequency = rope_base ** (
        -(jnp.arange(half_width, dtype=jnp.float32) * 2.0) / vectors.shape[-1]
    )
    angles = positions.astype(jnp.float32)[:, None] * frequency[None, :]
    cosine = jnp.cos(angles)[:, None, :]
    sine_part = jnp.sin(angles)[:, None, :]
    leading = vectors[..., :half_width]
    second = vectors[..., half_width:]
    return jnp.concatenate(
        [leading * cosine - second * sine_part, second * cosine + leading * sine_part], axis=-1
    )


def encode(normed, lengths_row, w_query, w_key, w_value):
    tok_count = normed.shape[0]
    query_count = lengths_row.shape[0]
    seq_ends = jnp.cumsum(lengths_row)
    starts = seq_ends - lengths_row
    places = jnp.arange(tok_count, dtype=jnp.int32)
    owners = jnp.sum((places[:, None] >= seq_ends[None, :]).astype(jnp.int32), axis=1)
    positions = places - jnp.take(starts, owners)
    finals = seq_ends - 1
    pooled = jnp.take(normed, finals, axis=0)
    kv_heads = w_key.shape[1] // HEAD
    q_heads = w_query.shape[1] // HEAD
    group_size = q_heads // kv_heads
    key_rows = jnp.dot(normed, w_key, preferred_element_type=jnp.float32).reshape(
        tok_count, kv_heads, HEAD
    )
    key_rows = rotate(key_rows, positions).astype(jnp.bfloat16)
    values = (
        jnp.dot(normed, w_value, preferred_element_type=jnp.float32)
        .astype(jnp.bfloat16)
        .reshape(tok_count, kv_heads, HEAD)
    )
    queries = jnp.dot(pooled, w_query, preferred_element_type=jnp.float32).reshape(
        query_count, q_heads, HEAD
    )
    queries = (
        rotate(queries, lengths_row - 1)
        .astype(jnp.bfloat16)
        .reshape(query_count, kv_heads, group_size, HEAD)
    )
    scores = jnp.einsum(
        "qgrd,tgd->grqt", queries, key_rows, preferred_element_type=jnp.float32
    ) * HEAD ** (-0.5)
    visible = (
        owners[None, None, None, :] == jnp.arange(query_count, dtype=jnp.int32)[None, None, :, None]
    )
    scores = jnp.where(visible, scores, -1e30)
    maxima = jnp.max(scores, axis=3, keepdims=True)
    weights = jnp.exp(scores - maxima)
    attn_probs = (weights / jnp.sum(weights, axis=3, keepdims=True)).astype(jnp.bfloat16)
    context = jnp.einsum("grqt,tgd->qgrd", attn_probs, values, preferred_element_type=jnp.float32)
    context = context.astype(jnp.bfloat16).reshape(query_count, q_heads * HEAD)
    return (context, finals)


def on_device(
    hidden,
    lengths,
    steer_ids,
    in_gain,
    w_query,
    w_key,
    w_value,
    w_out,
    steer_table,
    strength,
    out_gain,
    index_rows,
):
    group_rows = lax.all_gather(hidden, "tensor", axis=1, tiled=True)
    widened = group_rows.astype(jnp.float32)
    normed = (
        widened
        * lax.rsqrt(jnp.mean(widened * widened, axis=1, keepdims=True) + 1e-06)
        * in_gain[None, :]
    ).astype(jnp.bfloat16)
    context, finals = encode(normed, lengths[0], w_query, w_key, w_value)
    pooled_x = jnp.take(widened, finals, axis=0)
    one_hot = steer_ids[:, None] == jnp.arange(steer_table.shape[0], dtype=jnp.int32)[None, :]
    steering = jnp.dot(
        one_hot.astype(jnp.bfloat16), steer_table, preferred_element_type=jnp.float32
    )
    scaled = jnp.sum(jnp.where(one_hot, strength[None, :], 0.0), axis=1)
    partial_value = jnp.dot(context, w_out, preferred_element_type=jnp.float32)
    attn_out = lax.psum_scatter(partial_value, "tensor", scatter_dimension=1, tiled=True)
    local_width = attn_out.shape[1]
    column_start = lax.axis_index("tensor") * local_width
    residual = lax.dynamic_slice_in_dim(pooled_x, column_start, local_width, 1) + attn_out
    my_steering = lax.dynamic_slice_in_dim(steering, column_start, local_width, 1)
    my_gain = lax.dynamic_slice_in_dim(out_gain, column_start, local_width, 0)
    self_sq, steer_sq = lax.psum(
        (jnp.sum(residual * residual, axis=1), jnp.sum(my_steering * my_steering, axis=1)), "tensor"
    )
    factor = scaled * jnp.sqrt(self_sq / D / (steer_sq / D + 1e-06))
    gained = (residual + factor[:, None] * my_steering) * my_gain[None, :]
    totals = lax.psum(jnp.sum(gained * gained, axis=1), "tensor")
    local_embed = (gained * lax.rsqrt(totals + 1e-06)[:, None]).astype(jnp.bfloat16)
    embeddings = lax.all_gather(local_embed, "tensor", axis=1, tiled=True)
    return lax.dot_general(
        lax.all_gather(embeddings, "corpus", axis=0, tiled=True),
        index_rows,
        (((1,), (1,)), ((), ())),
        preferred_element_type=jnp.float32,
    ).astype(jnp.bfloat16)


def solution(mesh):
    placed = (
        P("corpus", "tensor"),
        P("corpus", None),
        P("corpus"),
        P(),
        P(None, "tensor"),
        P(None, "tensor"),
        P(None, "tensor"),
        P("tensor", None),
        P(),
        P(),
        P(),
        P(("corpus", "tensor"), None),
    )
    return jax.shard_map(
        on_device,
        mesh=mesh,
        in_specs=placed,
        out_specs=P(None, ("corpus", "tensor")),
        check_vma=False,
    )
```

profile of v0, /device:TPU:1, one launch (start us, length us, event | category | flops | bytes accessed | tf_op | source)
XLA Modules:
  0.0 206.8 jit_solution(14262951301222223644)
XLA Ops:
  6.5 0.7 all-gather.3.cloned.1.call-update
  7.3 0.0 reduce-scatter.2.cloned.1.call-start
  7.3 0.7 copy.26
  8.0 0.1 reduce-window.4
  8.1 0.1 fusion.23
  8.2 0.7 fusion.29
  8.9 0.7 fusion.49
  9.6 0.1 convert_reduce_fusion
  9.7 4.3 %fusion.28 = (s32[384]{0:T(512)S(1)}, s32[384,1]{0,1:T(1,128)S(1)}) fusion(s32[]{:T(128)} %bitcast.30, s32[]{:T(128)} %bitcast.31, s32[]{:T(128)} %bitcast.32, s32[]{:T(128)} %bitcast.33, s32[]{:T(128)} %bitcast.34, s32[]{:T(128)} %bitcast.36, s32[]{:T(128)} %bitcast.35, s32[384]{0:T(512)S(1)} %convert_reduce_fusion), kind=kLoop, calls=%fused_computation.90 | loop fusion | flops 5760 | bytes 4636 | tf_op jit(solution)/shard_map/jit(_take)/gather | solution.py:33
  14.0 0.7 fusion.48
  14.8 0.1 compare_reduce_fusion.24
  14.9 15.7 %fusion.27 = f32[384]{0:T(512)S(1)} fusion(pred[384]{0:T(512)(128)(4,1)S(1)} %get-tuple-element.31, pred[384]{0:T(512)(128)(4,1)S(1)} %get-tuple-element.30, pred[384]{0:T(512)(128)(4,1)S(1)} %get-tuple-element.29, pred[384]{0:T(512)(128)(4,1)S(1)} %get-tuple-element.28, pred[384]{0:T(512)(128)(4,1)S(1)} %get-tuple-element.27, ...), kind=kLoop, calls=%fused_computation.87 | loop fusion | flops 13056 | bytes 14308 | tf_op jit(solution)/shard_map/convert_element_type | solution.py:16
  30.6 0.1 multiply_cosine_fusion.1
  30.8 0.8 multiply_cosine_fusion
  31.5 20.0 %all-gather.3.cloned.1.call-done = bf16[384,4096]{1,0:T(8,128)(2,1)} async-done(((bf16[384,1024]{1,0:T(8,128)(2,1)}), bf16[384,4096]{1,0:T(8,128)(2,1)}) %all-gather.3.cloned.1.call-update) | async-done | bytes 3145744 | tf_op jit(solution)/shard_map/all_gather | solution.py:85
  51.6 2.7 %multiply_reduce_fusion = f32[384]{0:T(512)S(1)} fusion(bf16[384,4096]{1,0:T(8,128)(2,1)} %all-gather.3.cloned.1.call-done), kind=kLoop, calls=%fused_computation.4 | loop fusion | flops 4718208 | bytes 3147264 | tf_op jit(solution)/shard_map/reduce_sum | solution.py:89
  54.3 0.1 copy-done.1
  54.4 1.1 multiply_convert_fusion
  55.5 1.7 copy-done.2
  57.2 2.0 convolution_convert_fusion.1
  59.2 3.2 %gather_fusion.1 = bf16[32,4096]{1,0:T(8,128)(2,1)S(1)} fusion(bf16[384,4096]{1,0:T(8,128)(2,1)} %copy-done.2, s32[1024]{0:T(1024)S(1)} %pad_clamp_fusion), kind=kCustom, calls=%fused_computation.1 | custom fusion | bytes 524416 | tf_op jit(solution)/shard_map/jit(_take)/gather | solution.py:35
  62.4 4.7 %fusion.53 = f32[384,256]{0,1:T(8,128)} fusion(bf16[384,4096]{1,0:T(8,128)(2,1)} %copy-done.2, bf16[4096,256]{1,0:T(8,128)(2,1)} %param.17), kind=kOutput, calls=%fused_computation.112 | convolution fusion | flops 805306368 | bytes 5636096 | tf_op jit(solution)/shard_map/dot_general | solution.py:39
  67.2 0.9 fusion.6
  68.1 0.1 subtract_convert_fusion.1
  68.2 1.1 fusion.47
  69.3 0.2 copy.38
  69.4 0.2 copy.37
  69.6 0.8 subtract_convert_fusion
  70.4 1.4 fusion.50
  71.8 1.5 fusion.5
  73.4 3.8 %fusion.54 = f32[32,4096]{1,0:T(8,128)} fusion(bf16[32,512]{1,0:T(8,128)(2,1)S(1)} %reshape.233, bf16[512,4096]{1,0:T(8,128)(2,1)} %param.19), kind=kOutput, calls=%fused_computation.113 | convolution fusion | flops 134217728 | bytes 4751360 | tf_op jit(solution)/shard_map/dot_general | solution.py:99
  77.2 0.0 reduce-scatter.2.cloned.1.call-update
  77.2 0.0 all-gather.5.cloned.1.call-start
  77.3 0.3 fusion.24
  77.6 0.1 multiply_reduce_fusion.2
  77.7 0.1 select_reduce_fusion
  77.8 5.3 %convert_element_type.45 = f32[384,4096]{1,0:T(8,128)} convert(bf16[384,4096]{1,0:T(8,128)(2,1)} %all-gather.3.cloned.1.call-done) | non-fusion elementwise | flops 1572864 | bytes 9437184 | tf_op jit(solution)/shard_map/convert_element_type | solution.py:86
  83.1 3.8 %gather_fusion = f32[32,4096]{1,0:T(8,128)S(1)} fusion(f32[384,4096]{1,0:T(8,128)} %convert_element_type.45, s32[1024]{0:T(1024)S(1)} %pad_clamp_fusion), kind=kCustom, calls=%fused_computation | custom fusion | bytes 1048704 | tf_op jit(solution)/shard_map/jit(_take)/gather | solution.py:93
  86.9 10.1 %reduce-scatter.2.cloned.1.call-done = f32[32,1024]{1,0:T(8,128)} async-done(((f32[32,4096]{1,0:T(8,128)}), f32[32,1024]{1,0:T(8,128)}) %reduce-scatter.2.cloned.1.call-update) | async-done | bytes 131088 | tf_op jit(solution)/shard_map/reduce_scatter | solution.py:100
  96.9 1.1 multiply_reduce_fusion.3
  98.0 7.1 %all-reduce = (f32[32]{0:T(128)S(1)}, f32[32]{0:T(128)S(1)}) all-reduce(f32[32]{0:T(128)S(1)} %multiply_reduce_fusion.2, f32[32]{0:T(128)S(1)} %multiply_reduce_fusion.3), channel_id=1, replica_groups=mesh['corpus'=32,'tensor'=4] {'tensor'}, use_global_device_ids=true, to_apply=%region_10.11 | all-reduce | flops 64 | bytes 512 | tf_op jit(solution)/shard_map/psum | solution.py:106
  105.1 1.1 multiply_reduce_fusion.1
  106.2 6.4 %psum.23 = f32[32]{0:T(128)S(1)} all-reduce(f32[32]{0:T(128)S(1)} %get-tuple-element.34), channel_id=1, replica_groups=mesh['corpus'=32,'tensor'=4] {'tensor'}, use_global_device_ids=true, to_apply=%region_12.13 | all-reduce | flops 32 | bytes 256 | tf_op jit(solution)/shard_map/psum | solution.py:111
  112.6 0.1 multiply_convert_fusion.1
  112.7 10.3 %all_gather.10 = bf16[32,4096]{1,0:T(8,128)(2,1)} all-gather(bf16[32,1024]{1,0:T(8,128)(2,1)S(1)} %multiply_convert_fusion.1), channel_id=1, replica_groups=mesh['corpus'=32,'tensor'=4] {'tensor'}, dimensions={1}, use_global_device_ids=true | all-gather | bytes 327680 | tf_op jit(solution)/shard_map/all_gather | solution.py:113
  123.0 0.0 all-gather.5.cloned.1.call-update
  123.0 62.5 %all-gather.5.cloned.1.call-done = bf16[1024,4096]{1,0:T(8,128)(2,1)} async-done(((bf16[32,4096]{1,0:T(8,128)(2,1)}), bf16[1024,4096]{1,0:T(8,128)(2,1)}) %all-gather.5.cloned.1.call-update) | async-done | bytes 8388624 | tf_op jit(solution)/shard_map/all_gather | solution.py:115
  185.5 14.7 %convolution_convert_fusion = bf16[1024,1024]{1,0:T(8,128)(2,1)} fusion(bf16[1024,4096]{1,0:T(8,128)(2,1)} %all-gather.5.cloned.1.call-done, bf16[1024,4096]{1,0:T(8,128)(2,1)} %param.23), kind=kOutput, calls=%fused_computation.5 | convolution fusion | flops 8590983168 | bytes 18874368 | tf_op jit(solution)/shard_map/dot_general | solution.py:114
  (33 shorter events, 0.2 us)
Async XLA Ops:
  6.5 50.6 %copy-start = (bf16[4096,256]{1,0:T(8,128)(2,1)S(1)}, bf16[4096,256]{1,0:T(8,128)(2,1)}, u32[]{:S(2)}) copy-start(bf16[4096,256]{1,0:T(8,128)(2,1)} %param.18) | copy-start | bytes 6291460
  6.5 47.8 %copy-start.5 = (f32[4096]{0:T(1024)S(1)}, f32[4096]{0:T(1024)}, u32[]{:S(2)}) copy-start(f32[4096]{0:T(1024)} %param.15) | copy-start | bytes 49156
  6.5 45.0 %all-gather.3.cloned.1.call-start = ((), (), s32[]{:S(2)}) async-start(), calls=%async_computation.1 | async-start | bytes 3932160 | tf_op jit(solution)/shard_map/all_gather | solution.py:85
  7.3 89.7 %reduce-scatter.2.cloned.1.call-start = ((), (), s32[]{:S(2)}) async-start(), calls=%async_computation.2 | async-start | bytes 655360 | tf_op jit(solution)/shard_map/reduce_scatter | solution.py:100
  14.9 52.3 %copy-start.6 = (pred[32]{0:T(512)(128)(4,1)}, pred[32]{0:T(512)(128)(4,1)S(1)}, u32[]{:S(2)}) copy-start(pred[32]{0:T(512)(128)(4,1)S(1)} %compare_and_fusion) | copy-start | bytes 100
  51.6 2.8 %copy-start.1 = (bf16[384,4096]{1,0:T(8,128)(2,1)S(1)}, bf16[384,4096]{1,0:T(8,128)(2,1)}, u32[]{:S(2)}) copy-start(bf16[384,4096]{1,0:T(8,128)(2,1)} %all-gather.3.cloned.1.call-done) | copy-start | bytes 9437188
  55.5 1.7 copy-start.2
  62.4 4.7 %copy-start.3 = (bf16[4096,512]{1,0:T(8,128)(2,1)S(1)}, bf16[4096,512]{1,0:T(8,128)(2,1)}, u32[]{:S(2)}) copy-start(bf16[4096,512]{1,0:T(8,128)(2,1)} %param.16) | copy-start | bytes 12582916
  70.4 6.9 %copy-start.4 = (bf16[16,4096]{1,0:T(8,128)(2,1)S(1)}, bf16[16,4096]{1,0:T(8,128)(2,1)}, u32[]{:S(2)}) copy-start(bf16[16,4096]{1,0:T(8,128)(2,1)} %param.20) | copy-start | bytes 393220
  70.4 6.9 %copy-start.8 = (s32[32]{0:T(128)S(1)}, s32[32]{0:T(128)}, u32[]{:S(2)}) copy-start(s32[32]{0:T(128)} %param.14) | copy-start | bytes 388
  70.4 7.3 %copy-start.9 = (f32[16]{0:T(128)S(1)}, f32[16]{0:T(128)}, u32[]{:S(2)}) copy-start(f32[16]{0:T(128)} %param.21) | copy-start | bytes 196
  77.2 108.3 %all-gather.5.cloned.1.call-start = ((), (), s32[]{:S(2)}) async-start(), calls=%async_computation.3 | async-start | bytes 8650752 | tf_op jit(solution)/shard_map/all_gather | solution.py:115
  83.1 13.8 %copy-start.7 = (pred[32]{0:T(512)(128)(4,1)S(1)}, pred[32]{0:T(512)(128)(4,1)}, u32[]{:S(2)}) copy-start(pred[32]{0:T(512)(128)(4,1)} %copy-done.6) | copy-start | bytes 100
  83.1 22.0 %dynamic-slice-start = ((f32[4096]{0:T(1024)}, s32[]{:T(128)}), f32[1024]{0:T(1024)S(1)}, s32[]{:S(2)}) async-start(f32[4096]{0:T(1024)} %param.22, s32[]{:T(128)} %select_n.69), calls=%async_computation.4 | async-start | bytes 8704 | tf_op jit(solution)/shard_map/dynamic_slice | solution.py:105
Sparse Core Ops, SparseCore 0:
  9.0 42.5 all-gather.2
  77.4 19.5 reduce-scatter.1
  123.2 62.3 all-gather.4
where the time goes:
time: 207 us
  waiting for transfers between devices  93.3 us (45%)
  other arithmetic  34.6 us (17%)
  matrix products  29.3 us (14%)
  blocking collectives  23.7 us (11%)
  between operations  13.3 us (6%)
  local copies, waits for them, and re-layouts  12.4 us (6%)
    all_gather x1, waiting for transfers between devices, on_device(): lax.all_gather(embeddings, 'corpus', axis=0, tiled=True)  62.5 us
    all_gather x1, waiting for transfers between devices, on_device(): group_rows = lax.all_gather(hidden, 'tensor', axis=1, tiled=True)  20 us
    convert_element_type x2, other arithmetic, rotate(): angles = positions.astype(jnp.float32)[:, None] * frequency[None, :]  16.4 us
    dot_general x1, matrix products, on_device(): lax.dot_general(lax.all_gather(embeddings, 'corpus', axis=0, tiled=True),...  14.7 us
    all_gather x1, blocking collectives, on_device(): embeddings = lax.all_gather(local_embed, 'tensor', axis=1, tiled=True)  10.3 us
    reduce_scatter x1, waiting for transfers between devices, on_device(): lax.psum_scatter(partial_value, 'tensor', scatter_dimension=1, tiled=True)  10.1 us
    psum x1, blocking collectives, on_device(): lax.psum((jnp.sum(residual * residual, axis=1), jnp.sum(my_steering * my_...  7.05 us
    psum x1, blocking collectives, on_device(): totals = lax.psum(jnp.sum(gained * gained, axis=1), 'tensor')  6.39 us
  transfers between devices with their start and end apart: 3, of which 3 were waited for; matrix products, arithmetic and copies ran while one was open for 16% of the time, Pallas kernels for 0%

commit v1 on v0

--- a/solution.py
+++ b/solution.py
@@ -112,7 +112,10 @@
     local_embed = (gained * lax.rsqrt(totals + 1e-06)[:, None]).astype(jnp.bfloat16)
     embeddings = lax.all_gather(local_embed, "tensor", axis=1, tiled=True)
     return lax.dot_general(
-        lax.all_gather(embeddings, "corpus", axis=0, tiled=True),
+        jnp.concatenate(
+            lax.all_to_all(jnp.stack([embeddings] * lax.axis_size("corpus")), "corpus", 0, 0),
+            axis=0,
+        ),
         index_rows,
         (((1,), (1,)), ((), ())),
         preferred_element_type=jnp.float32,

time: 207 us -> 255 us (1.23)
  blocking collectives: 23.7 us -> 135 us
  waiting for transfers between devices: 93.3 us -> 30.8 us
    all_to_all x0 -> x1, blocking collectives: none -> 112 us  [on_device(): lax.all_to_all(jnp.stack([embeddings] * lax.axis_size('corpus')), 'corpus...]
    all_gather x1 -> x0, waiting for transfers between devices: 62.5 us -> none  [on_device(): lax.all_gather(embeddings, 'corpus', axis=0, tiled=True)]
  transfers between devices with their start and end apart: 3 -> 2, of which waited for: 3 -> 2; matrix products, arithmetic and copies ran while one was open for 16% -> 13% of each run, Pallas kernels for 0% -> 0%
where the time goes in v1:
time: 255 us
  blocking collectives  135 us (53%)
  other arithmetic  34.6 us (14%)
  waiting for transfers between devices  30.8 us (12%)
  matrix products  26.8 us (11%)
  between operations  13.6 us (5%)
  local copies, waits for them, and re-layouts  13.5 us (5%)
    all_to_all x1, blocking collectives, on_device(): lax.all_to_all(jnp.stack([embeddings] * lax.axis_size('corpus')), 'corpus...  112 us
    all_gather x1, waiting for transfers between devices, on_device(): group_rows = lax.all_gather(hidden, 'tensor', axis=1, tiled=True)  20 us
    convert_element_type x2, other arithmetic, rotate(): angles = positions.astype(jnp.float32)[:, None] * frequency[None, :]  16.4 us
    dot_general x1, matrix products, on_device(): lax.dot_general(jnp.concatenate(lax.all_to_all(jnp.stack([embeddings] * l...  12.2 us
    reduce_scatter x1, waiting for transfers between devices, on_device(): lax.psum_scatter(partial_value, 'tensor', scatter_dimension=1, tiled=True)  10.1 us
    all_gather x1, blocking collectives, on_device(): embeddings = lax.all_gather(local_embed, 'tensor', axis=1, tiled=True)  9.36 us
    psum x1, blocking collectives, on_device(): lax.psum((jnp.sum(residual * residual, axis=1), jnp.sum(my_steering * my_...  7.05 us
    psum x1, blocking collectives, on_device(): totals = lax.psum(jnp.sum(gained * gained, axis=1), 'tensor')  6.39 us
  transfers between devices with their start and end apart: 2, of which 2 were waited for; matrix products, arithmetic and copies ran while one was open for 13% of the time, Pallas kernels for 0%

profile of v1, /device:TPU:1, one launch (start us, length us, event | category | flops | bytes accessed | tf_op | source)
XLA Modules:
  0.0 254.6 jit_solution(16187978500825321272)
XLA Ops:
  6.5 0.7 all-gather.2.cloned.1.call-update
  7.3 0.0 reduce-scatter.2.cloned.1.call-start
  7.3 0.7 copy.26
  8.0 0.1 reduce-window.4
  8.1 0.1 fusion.23
  8.2 0.7 fusion.29
  8.9 0.7 fusion.49
  9.6 0.1 convert_reduce_fusion
  9.7 4.3 %fusion.28 = (s32[384]{0:T(512)S(1)}, s32[384,1]{0,1:T(1,128)S(1)}) fusion(s32[]{:T(128)} %bitcast.30, s32[]{:T(128)} %bitcast.31, s32[]{:T(128)} %bitcast.32, s32[]{:T(128)} %bitcast.33, s32[]{:T(128)} %bitcast.34, s32[]{:T(128)} %bitcast.36, s32[]{:T(128)} %bitcast.35, s32[384]{0:T(512)S(1)} %convert_reduce_fusion), kind=kLoop, calls=%fused_computation.90 | loop fusion | flops 5760 | bytes 4636 | tf_op jit(solution)/shard_map/jit(_take)/gather | solution.py:33
  14.0 0.7 fusion.48
  14.8 0.1 compare_reduce_fusion.24
  14.9 15.7 %fusion.27 = f32[384]{0:T(512)S(1)} fusion(pred[384]{0:T(512)(128)(4,1)S(1)} %get-tuple-element.31, pred[384]{0:T(512)(128)(4,1)S(1)} %get-tuple-element.30, pred[384]{0:T(512)(128)(4,1)S(1)} %get-tuple-element.29, pred[384]{0:T(512)(128)(4,1)S(1)} %get-tuple-element.28, pred[384]{0:T(512)(128)(4,1)S(1)} %get-tuple-element.27, ...), kind=kLoop, calls=%fused_computation.87 | loop fusion | flops 13056 | bytes 14308 | tf_op jit(solution)/shard_map/convert_element_type | solution.py:16
  30.6 0.1 multiply_cosine_fusion.1
  30.8 0.8 multiply_cosine_fusion
  31.5 20.0 %all-gather.2.cloned.1.call-done = bf16[384,4096]{1,0:T(8,128)(2,1)} async-done(((bf16[384,1024]{1,0:T(8,128)(2,1)}), bf16[384,4096]{1,0:T(8,128)(2,1)}) %all-gather.2.cloned.1.call-update) | async-done | bytes 3145744 | tf_op jit(solution)/shard_map/all_gather | solution.py:85
  51.6 2.7 %multiply_reduce_fusion = f32[384]{0:T(512)S(1)} fusion(bf16[384,4096]{1,0:T(8,128)(2,1)} %all-gather.2.cloned.1.call-done), kind=kLoop, calls=%fused_computation.4 | loop fusion | flops 4718208 | bytes 3147264 | tf_op jit(solution)/shard_map/reduce_sum | solution.py:89
  54.3 0.1 copy-done.1
  54.4 1.1 multiply_convert_fusion
  55.5 1.7 copy-done.2
  57.2 2.0 convolution_convert_fusion.1
  59.2 3.2 %gather_fusion.1 = bf16[32,4096]{1,0:T(8,128)(2,1)S(1)} fusion(bf16[384,4096]{1,0:T(8,128)(2,1)} %copy-done.2, s32[1024]{0:T(1024)S(1)} %pad_clamp_fusion), kind=kCustom, calls=%fused_computation.1 | custom fusion | bytes 524416 | tf_op jit(solution)/shard_map/jit(_take)/gather | solution.py:35
  62.4 0.0 copy-start.3
  62.4 4.7 %fusion.53 = f32[384,256]{0,1:T(8,128)} fusion(bf16[384,4096]{1,0:T(8,128)(2,1)} %copy-done.2, bf16[4096,256]{1,0:T(8,128)(2,1)} %param.17), kind=kOutput, calls=%fused_computation.112 | convolution fusion | flops 805306368 | bytes 5636096 | tf_op jit(solution)/shard_map/dot_general | solution.py:39
  67.2 0.9 fusion.6
  68.1 0.1 subtract_convert_fusion.1
  68.2 1.1 fusion.47
  69.3 0.2 copy.38
  69.4 0.2 copy.37
  69.6 0.8 subtract_convert_fusion
  70.4 1.4 fusion.50
  71.8 1.5 fusion.5
  73.4 3.8 %fusion.54 = f32[32,4096]{1,0:T(8,128)} fusion(bf16[32,512]{1,0:T(8,128)(2,1)S(1)} %reshape.238, bf16[512,4096]{1,0:T(8,128)(2,1)} %param.19), kind=kOutput, calls=%fused_computation.113 | convolution fusion | flops 134217728 | bytes 4751360 | tf_op jit(solution)/shard_map/dot_general | solution.py:99
  77.2 0.0 reduce-scatter.2.cloned.1.call-update
  77.3 0.3 fusion.24
  77.5 0.1 multiply_reduce_fusion.2
  77.7 0.1 select_reduce_fusion
  77.8 5.3 %convert_element_type.45 = f32[384,4096]{1,0:T(8,128)} convert(bf16[384,4096]{1,0:T(8,128)(2,1)} %all-gather.2.cloned.1.call-done) | non-fusion elementwise | flops 1572864 | bytes 9437184 | tf_op jit(solution)/shard_map/convert_element_type | solution.py:86
  83.1 3.8 %gather_fusion = f32[32,4096]{1,0:T(8,128)S(1)} fusion(f32[384,4096]{1,0:T(8,128)} %convert_element_type.45, s32[1024]{0:T(1024)S(1)} %pad_clamp_fusion), kind=kCustom, calls=%fused_computation | custom fusion | bytes 1048704 | tf_op jit(solution)/shard_map/jit(_take)/gather | solution.py:93
  86.8 10.1 %reduce-scatter.2.cloned.1.call-done = f32[32,1024]{1,0:T(8,128)} async-done(((f32[32,4096]{1,0:T(8,128)}), f32[32,1024]{1,0:T(8,128)}) %reduce-scatter.2.cloned.1.call-update) | async-done | bytes 131088 | tf_op jit(solution)/shard_map/reduce_scatter | solution.py:100
  96.9 1.1 multiply_reduce_fusion.3
  98.0 7.1 %all-reduce = (f32[32]{0:T(128)S(1)}, f32[32]{0:T(128)S(1)}) all-reduce(f32[32]{0:T(128)S(1)} %multiply_reduce_fusion.2, f32[32]{0:T(128)S(1)} %multiply_reduce_fusion.3), channel_id=1, replica_groups=mesh['corpus'=32,'tensor'=4] {'tensor'}, use_global_device_ids=true, to_apply=%region_10.11 | all-reduce | flops 64 | bytes 512 | tf_op jit(solution)/shard_map/psum | solution.py:106
  105.1 1.1 multiply_reduce_fusion.1
  106.2 6.4 %psum.23 = f32[32]{0:T(128)S(1)} all-reduce(f32[32]{0:T(128)S(1)} %get-tuple-element.34), channel_id=1, replica_groups=mesh['corpus'=32,'tensor'=4] {'tensor'}, use_global_device_ids=true, to_apply=%region_12.13 | all-reduce | flops 32 | bytes 256 | tf_op jit(solution)/shard_map/psum | solution.py:111
  112.6 0.1 multiply_convert_fusion.1
  112.7 9.4 %all_gather.7 = bf16[32,4096]{1,0:T(8,128)(2,1)S(1)} all-gather(bf16[32,1024]{1,0:T(8,128)(2,1)S(1)} %multiply_convert_fusion.1), channel_id=1, replica_groups=mesh['corpus'=32,'tensor'=4] {'tensor'}, dimensions={1}, use_global_device_ids=true | all-gather | bytes 327680 | tf_op jit(solution)/shard_map/all_gather | solution.py:113
  122.1 1.0 stack.2
  123.1 112.4 %all_to_all.5 = bf16[32,32,4096]{2,1,0:T(8,128)(2,1)S(1)} all-to-all(bf16[32,32,4096]{2,1,0:T(8,128)(2,1)S(1)} %stack.2), channel_id=1, replica_groups=mesh['corpus'=32,'tensor'=4] {'corpus'}, dimensions={0} | all-to-all | bytes 16777216 | tf_op jit(solution)/shard_map/all_to_all | solution.py:116
  235.5 12.2 %convolution_convert_fusion = bf16[1024,1024]{1,0:T(8,128)(2,1)} fusion(bf16[1024,4096]{1,0:T(8,128)(2,1)S(1)} %bitcast.89, bf16[1024,4096]{1,0:T(8,128)(2,1)} %param.23), kind=kOutput, calls=%fused_computation.5 | convolution fusion | flops 8590983168 | bytes 18874368 | tf_op jit(solution)/shard_map/dot_general | solution.py:114
  (32 shorter events, 0.2 us)
Async XLA Ops:
  6.5 50.6 %copy-start = (bf16[4096,256]{1,0:T(8,128)(2,1)S(1)}, bf16[4096,256]{1,0:T(8,128)(2,1)}, u32[]{:S(2)}) copy-start(bf16[4096,256]{1,0:T(8,128)(2,1)} %param.18) | copy-start | bytes 6291460
  6.5 47.8 %copy-start.5 = (f32[4096]{0:T(1024)S(1)}, f32[4096]{0:T(1024)}, u32[]{:S(2)}) copy-start(f32[4096]{0:T(1024)} %param.15) | copy-start | bytes 49156
  6.5 45.0 %all-gather.2.cloned.1.call-start = ((), (), s32[]{:S(2)}) async-start(), calls=%async_computation.2 | async-start | bytes 3932160 | tf_op jit(solution)/shard_map/all_gather | solution.py:85
  7.3 89.7 %reduce-scatter.2.cloned.1.call-start = ((), (), s32[]{:S(2)}) async-start(), calls=%async_computation.3 | async-start | bytes 655360 | tf_op jit(solution)/shard_map/reduce_scatter | solution.py:100
  14.9 52.3 %copy-start.6 = (pred[32]{0:T(512)(128)(4,1)}, pred[32]{0:T(512)(128)(4,1)S(1)}, u32[]{:S(2)}) copy-start(pred[32]{0:T(512)(128)(4,1)S(1)} %compare_and_fusion) | copy-start | bytes 100
  51.6 2.8 %copy-start.1 = (bf16[384,4096]{1,0:T(8,128)(2,1)S(1)}, bf16[384,4096]{1,0:T(8,128)(2,1)}, u32[]{:S(2)}) copy-start(bf16[384,4096]{1,0:T(8,128)(2,1)} %all-gather.2.cloned.1.call-done) | copy-start | bytes 9437188
  55.5 1.7 copy-start.2
  62.4 4.7 %copy-start.3 = (bf16[4096,512]{1,0:T(8,128)(2,1)S(1)}, bf16[4096,512]{1,0:T(8,128)(2,1)}, u32[]{:S(2)}) copy-start(bf16[4096,512]{1,0:T(8,128)(2,1)} %param.16) | copy-start | bytes 12582916
  70.4 6.9 %copy-start.4 = (bf16[16,4096]{1,0:T(8,128)(2,1)S(1)}, bf16[16,4096]{1,0:T(8,128)(2,1)}, u32[]{:S(2)}) copy-start(bf16[16,4096]{1,0:T(8,128)(2,1)} %param.20) | copy-start | bytes 393220
  70.4 6.9 %copy-start.8 = (s32[32]{0:T(128)S(1)}, s32[32]{0:T(128)}, u32[]{:S(2)}) copy-start(s32[32]{0:T(128)} %param.14) | copy-start | bytes 388
  70.4 7.3 %copy-start.9 = (f32[16]{0:T(128)S(1)}, f32[16]{0:T(128)}, u32[]{:S(2)}) copy-start(f32[16]{0:T(128)} %param.21) | copy-start | bytes 196
  83.1 13.9 %copy-start.7 = (pred[32]{0:T(512)(128)(4,1)S(1)}, pred[32]{0:T(512)(128)(4,1)}, u32[]{:S(2)}) copy-start(pred[32]{0:T(512)(128)(4,1)} %copy-done.6) | copy-start | bytes 100
  83.1 22.0 %dynamic-slice-start = ((f32[4096]{0:T(1024)}, s32[]{:T(128)}), f32[1024]{0:T(1024)S(1)}, s32[]{:S(2)}) async-start(f32[4096]{0:T(1024)} %param.22, s32[]{:T(128)} %select_n.69), calls=%async_computation.4 | async-start | bytes 8704 | tf_op jit(solution)/shard_map/dynamic_slice | solution.py:105
Sparse Core Ops, SparseCore 0:
  9.0 42.5 all-gather.1
  77.4 19.5 reduce-scatter.1
